TPU v7x, 256 devices: a whole 4x4x8 slice. The times are simulated.
256 devices in a mesh: req: 4 (over z_lo, core), exp: 64 (over y, x, z_hi).
Axes of the slice: x: 4, y: 4, z: 8 (z_hi: 4, z_lo: 2; z = z_hi * 2 + z_lo), core: 2. Of those that a mesh axis runs over, the one named last changes fastest.
Arguments:
- residual: bfloat16 [8192, 2048], P('exp'), may hold values from -6 to 6
- queries: bfloat16 [8192, 2048], P('exp', 'req'), may hold values from -128 to 128, as said below
- prefix_kv: bfloat16 [4, 16384, 256], P('req', 'exp'), may hold values from -4.5 to 4.5
- suffix_kv: bfloat16 [8192, 4, 256], P('exp', 'req'), may hold values from -6 to 6
- suffix_lengths: int32 [64, 4], P('exp'), may hold values from 1 to 96, 128 in all within a row
- out_proj: bfloat16 [2048, 2048], P('req'), may hold values from -0.5 to 0.5
- norm_gain: bfloat16 [2048], replicated, may hold values from 0.099609375 to 1.8984375
- routes: int32 [8192, 6], P('exp'), may hold values from 0 to 63, all different within a row; in each aligned block of 128 rows (0 to 127, 128 to 255, ...) at most 24 rows name the same one
- route_weights: float32 [8192, 6], P('exp'), may hold values from 0.1 to 0.5
- expert_gate: bfloat16 [64, 2048, 1408], P('exp', None, 'req'), may hold values from -0.125 to 0.125
- expert_up: bfloat16 [64, 2048, 1408], P('exp', None, 'req'), may hold values from -0.125 to 0.125
- expert_down: bfloat16 [64, 1408, 2048], P('exp', 'req'), may hold values from -0.15625 to 0.15625
- shared_gate: bfloat16 [2048, 1408], P(None, 'req'), may hold values from -0.125 to 0.125
- shared_up: bfloat16 [2048, 1408], P(None, 'req'), may hold values from -0.125 to 0.125
- shared_down: bfloat16 [1408, 2048], P('req'), may hold values from -0.15625 to 0.15625
Outputs:
- layer_out: bfloat16 [8192, 2048], P('exp')
Inputs may be any that keep to these rules, and one draw needn't show every extreme that they name: In the hidden draw some queries are strong multiples of prefix keys. `suffix_lengths`: each row (the requests of one index of exp) sums to 128, and in every row one request has exactly 96 tokens. `routes`: the 6 experts of a token are different. Among the 128 tokens of one index of exp no expert is picked more than 24 times, and in every draw some expert is picked exactly 24 times by the tokens of some index of exp.
All inputs are finite; a program needn't handle non-finite values.
Results may differ from a plain program's by a relative error of at most 0.015.
Values may be sent and summed in bfloat16 or wider, within the bound.
A program may use at most 128 MiB of HBM per device.

v0:
```python
import math
import jax
import jax.numpy as jnp
from jax import lax
from jax.sharding import PartitionSpec as P

HD = 128
TOP = 6
neg_big = -1e30
norm_eps = 1e-06


def on_device(
    residual,
    queries,
    prefix_kv,
    suffix_kv,
    suffix_lengths,
    out_proj,
    norm_gain,
    routes,
    route_weights,
    expert_gate,
    expert_up,
    expert_down,
    shared_gate,
    shared_up,
    shared_down,
):
    tokens_here = residual.shape[0]
    feat_width = residual.shape[1]
    head_count = queries.shape[1] // HD
    scaling = 1.0 / math.sqrt(HD)
    query_heads = jnp.transpose(queries.reshape(tokens_here, head_count, HD), (1, 0, 2))
    start_state = (
        jnp.full((head_count, tokens_here), neg_big, jnp.float32),
        jnp.zeros((head_count, tokens_here), jnp.float32),
        jnp.zeros((head_count, tokens_here, HD), jnp.float32),
    )

    def absorb(carried, key_rows, value_rows, allowed):
        running_max, running_sum, running_acc = carried
        scores = (
            jnp.einsum("htd,kd->htk", query_heads, key_rows, preferred_element_type=jnp.float32)
            * scaling
        )
        if allowed is not None:
            scores = jnp.where(allowed[None], scores, neg_big)
        new_max = jnp.maximum(running_max, jnp.max(scores, axis=-1))
        factor = jnp.exp(running_max - new_max)
        exp_scores = jnp.exp(scores - new_max[..., None])
        new_sum = running_sum * factor + jnp.sum(exp_scores, axis=-1)
        new_acc = running_acc * factor[..., None] + jnp.einsum(
            "htk,kd->htd",
            exp_scores.astype(jnp.bfloat16),
            value_rows,
            preferred_element_type=jnp.float32,
        )
        return (new_max, new_sum, new_acc)

    portion = lax.all_gather(prefix_kv, "exp", axis=1, tiled=True)
    key_count = portion.shape[1]
    window_len = math.gcd(key_count, 2048)

    def inner(position, inner_state):
        window = lax.dynamic_slice_in_dim(portion[0], position * window_len, window_len, 0)
        return absorb(inner_state, window[:, :HD], window[:, HD:], None)

    carried = lax.fori_loop(0, key_count // window_len, inner, start_state)
    request_ends = jnp.cumsum(suffix_lengths[0])
    positions = jnp.arange(tokens_here, dtype=jnp.int32)
    request_ids = jnp.sum((positions[:, None] >= request_ends[None, :]).astype(jnp.int32), axis=1)
    allowed = (request_ids[:, None] == request_ids[None, :]) & (
        positions[None, :] <= positions[:, None]
    )
    carried = absorb(carried, suffix_kv[:, 0, :HD], suffix_kv[:, 0, HD:], allowed)
    running_max, running_sum, running_acc = carried
    attention = (
        jnp.transpose(running_acc / running_sum[..., None], (1, 0, 2))
        .reshape(tokens_here, head_count * HD)
        .astype(jnp.bfloat16)
    )
    attn_terms = jnp.dot(attention, out_proj, preferred_element_type=jnp.float32)
    attn_out = lax.psum(attn_terms.astype(jnp.bfloat16), "req").astype(jnp.float32)
    hidden_state = (residual.astype(jnp.float32) + attn_out).astype(jnp.bfloat16)
    hidden_float = hidden_state.astype(jnp.float32)
    mean_square = jnp.mean(hidden_float * hidden_float, axis=-1, keepdims=True)
    normed = (
        hidden_float * lax.rsqrt(mean_square + norm_eps) * norm_gain.astype(jnp.float32)
    ).astype(jnp.bfloat16)
    shared_gate_act = jnp.dot(normed, shared_gate, preferred_element_type=jnp.float32)
    shared_up_act = jnp.dot(normed, shared_up, preferred_element_type=jnp.float32)
    shared_hidden = (jax.nn.silu(shared_gate_act) * shared_up_act).astype(jnp.bfloat16)
    shared_part = jnp.dot(shared_hidden, shared_down, preferred_element_type=jnp.float32)
    exp_count = lax.axis_size("exp")
    experts = exp_count * expert_gate.shape[0]
    capacity = min(tokens_here, 4 * ((tokens_here * TOP + 2 * experts - 1) // (2 * experts)))
    pick_ids = routes.reshape(-1)
    one_hot = (pick_ids[:, None] == jnp.arange(experts, dtype=jnp.int32)[None, :]).astype(jnp.int32)
    pick_ranks = jnp.sum((jnp.cumsum(one_hot, axis=0) - one_hot) * one_hot, axis=1)
    pick_slots = (pick_ids * capacity + pick_ranks).reshape(tokens_here, TOP)
    slot_ids = jnp.arange(experts * capacity, dtype=jnp.int32)
    placement = jnp.any(pick_slots[None, :, :] == slot_ids[:, None, None], axis=2).astype(
        jnp.bfloat16
    )
    buffer = (
        jnp.dot(placement, normed, preferred_element_type=jnp.float32)
        .astype(jnp.bfloat16)
        .reshape(experts, capacity, feat_width)
    )
    source_rows = lax.all_to_all(buffer, "exp", split_axis=0, concat_axis=0, tiled=True)
    sources, slot_count, row_width = source_rows.shape
    flat_rows = source_rows.reshape(sources * slot_count, row_width)
    gate_act = jnp.dot(flat_rows, expert_gate[0], preferred_element_type=jnp.float32)
    up_act = jnp.dot(flat_rows, expert_up[0], preferred_element_type=jnp.float32)
    expert_hidden = (jax.nn.silu(gate_act) * up_act).astype(jnp.bfloat16)
    partial_out = jnp.dot(expert_hidden, expert_down[0], preferred_element_type=jnp.float32).astype(
        jnp.bfloat16
    )
    finish_partial_out = partial_out.reshape(sources, slot_count, row_width)
    returned = lax.all_to_all(finish_partial_out, "exp", split_axis=0, concat_axis=0, tiled=True)
    flat_back = returned.reshape(experts * capacity, feat_width)
    picked_rows = (
        flat_back[pick_slots.reshape(-1)].astype(jnp.float32).reshape(tokens_here, TOP, feat_width)
    )
    routed = jnp.sum(picked_rows * route_weights[:, :, None], axis=1)
    summed = lax.psum((shared_part + routed).astype(jnp.bfloat16), "req").astype(jnp.float32)
    return (hidden_float + summed).astype(jnp.bfloat16)


def solution(mesh):
    placed = (
        P("exp", None),
        P("exp", "req"),
        P("req", "exp", None),
        P("exp", "req", None),
        P("exp", None),
        P("req", None),
        P(),
        P("exp", None),
        P("exp", None),
        P("exp", None, "req"),
        P("exp", None, "req"),
        P("exp", "req", None),
        P(None, "req"),
        P(None, "req"),
        P("req", None),
    )
    return jax.shard_map(
        on_device, mesh=mesh, in_specs=placed, out_specs=P("exp", None), check_vma=False
    )
```

profile of v0, /device:TPU:1, one launch (start us, length us, event | category | flops | bytes accessed | tf_op | source)
XLA Modules:
  0.0 634.4 jit_solution(8159375901670634559)
XLA Ops:
  14.6 2.2 fusion.53
  16.8 104.8 %all-gather.2.cloned.1.call-done = bf16[1,16384,256]{2,1,0:T(8,128)(2,1)} async-done(((bf16[1,256,256]{2,1,0:T(8,128)(2,1)}), bf16[1,16384,256]{2,1,0:T(8,128)(2,1)}) %all-gather.2.cloned.1.call-update) | async-done | bytes 8388624 | tf_op jit(solution)/shard_map/all_gather | solution.py:61
  121.6 67.1 %while.18 = (s32[]{:T(128)}, f32[4,128]{1,0:T(4,128)S(1)}, f32[4,128]{1,0:T(4,128)S(1)}, f32[4,128,128]{2,1,0:T(8,128)S(1)}, bf16[1,16384,256]{2,1,0:T(8,128)(2,...) while((s32[]{:T(128)}, f32[4,128]{1,0:T(4,128)S(1)}, ...), condition=%wide.region_3.0_spmd.clone, body=%wide.region_0.0_spmd.clone.sunk | while | flops 545458688 | bytes 33194172 | solution.py:69
  122.9 2.7 bitcast_reduce_fusion.2
  125.6 3.0 fusion.75
  131.3 2.7 bitcast_reduce_fusion.2
  134.0 3.0 fusion.75
  139.7 2.7 bitcast_reduce_fusion.2
  142.4 3.0 fusion.75
  148.1 2.7 bitcast_reduce_fusion.2
  150.8 3.0 fusion.75
  156.5 2.7 bitcast_reduce_fusion.2
  159.2 3.0 fusion.75
  164.9 2.7 bitcast_reduce_fusion.2
  167.6 3.0 fusion.75
  173.2 2.7 bitcast_reduce_fusion.2
  175.9 3.0 fusion.75
  181.6 2.7 bitcast_reduce_fusion.2
  184.3 3.0 fusion.75
  194.4 48.7 %all-reduce.3.cloned.1.call-done = bf16[128,2048]{1,0:T(8,128)(2,1)} async-done(((bf16[128,2048]{1,0:T(8,128)(2,1)}), bf16[128,2048]{1,0:T(8,128)(2,1)}) %all-reduce.3.cloned.1.call-update) | async-done | bytes 524304 | tf_op jit(solution)/shard_map/psum | solution.py:84
  247.5 126.4 %all_to_all.10 = bf16[64,24,2048]{2,1,0:T(8,128)(2,1)S(1)} all-to-all(bf16[64,24,2048]{2,1,0:T(8,128)(2,1)S(1)} %bitcast.103), channel_id=1, replica_groups=mesh['req'=4,'exp'=64] {'exp'}, dimensions={0} | all-to-all | bytes 12582912 | tf_op jit(solution)/shard_map/all_to_all | solution.py:111
  373.9 2.7 copy-done.3
  376.6 3.8 fusion.18
  380.4 12.3 %convolution_convert_fusion = bf16[1536,2048]{1,0:T(8,128)(2,1)} fusion(bf16[1,352,2048]{2,1,0:T(8,128)(2,1)} %param.28, bf16[1536,2048]{1,0:T(8,128)(2,1)} %bitcast.106, f32[1536,352]{0,1:T(8,128)} %fusion.18, bf16[1,2048,352]{1,2,0:T(8,128)(2,1)} %param.27), kind=kOutput, calls=%fused_computation.21 | convolution fusion | flops 4435574784 | bytes 17629184 | tf_op jit(solution)/shard_map/dot_general | solution.py:117
  392.7 8.7 %all-to-all-start.1 = ((bf16[64,24,2048]{2,1,0:T(8,128)(2,1)}), bf16[64,24,2048]{2,1,0:T(8,128)(2,1)}, u32[]{:S(2)}, u32[]{:S(2)}) async-start(bf16[64,24,2048]{2,1,0:T(8,128)(2,1)} %bitcast.104), calls=%async_computation.1 | async-start | bytes 12582912 | tf_op jit(solution)/shard_map/all_to_all | solution.py:121
  402.5 139.7 %all-to-all-done.1 = bf16[64,24,2048]{2,1,0:T(8,128)(2,1)} async-done(((bf16[64,24,2048]{2,1,0:T(8,128)(2,1)}), bf16[64,24,2048]{2,1,0:T(8,128)(2,1)}, u32[]{:S(2)}, u32[]{:S(2)}) %all-to-all-start.1) | async-done | bytes 6291488 | tf_op jit(solution)/shard_map/all_to_all | solution.py:121
  542.2 10.7 %gather_fusion = bf16[768,2048]{1,0:T(8,128)(2,1)} fusion(bf16[1536,2048]{1,0:T(8,128)(2,1)} %bitcast.18, s32[1024]{0:T(1024)S(1)} %pad_clamp_fusion), kind=kCustom, calls=%fused_computation | custom fusion | bytes 6294528 | tf_op jit(solution)/shard_map/gather | solution.py:124
  552.9 6.6 %reshape.163 = f32[128,6,2048]{2,1,0:T(8,128)} reshape(bf16[768,2048]{1,0:T(8,128)(2,1)} %gather_fusion) | data formatting | bytes 9437184 | tf_op jit(solution)/shard_map/convert_element_type | solution.py:124
  559.5 7.6 %multiply_reduce_fusion = f32[128,2048]{1,0:T(8,128)} fusion(f32[128,6,2048]{2,1,0:T(8,128)} %reshape.163, f32[128,6]{1,0:T(8,128)S(1)} %copy.46), kind=kLoop, calls=%fused_computation.20 | loop fusion | flops 2883584 | bytes 7343104 | tf_op jit(solution)/shard_map/reduce_sum | solution.py:126
  567.1 4.5 fusion.15
  571.6 54.0 %all-reduce.5.cloned.1.call-done = bf16[128,2048]{1,0:T(8,128)(2,1)} async-done(((bf16[128,2048]{1,0:T(8,128)(2,1)}), bf16[128,2048]{1,0:T(8,128)(2,1)}) %all-reduce.5.cloned.1.call-update) | async-done | bytes 524304 | tf_op jit(solution)/shard_map/psum | solution.py:127
  625.7 2.2 fusion.27
  (123 shorter events, 39.9 us)
Async XLA Ops:
  6.5 185.3 %copy-start = (bf16[512,2048]{1,0:T(8,128)(2,1)S(1)}, bf16[512,2048]{1,0:T(8,128)(2,1)}, u32[]{:S(2)}) copy-start(bf16[512,2048]{1,0:T(8,128)(2,1)} %param.22) | copy-start | bytes 6291460
  6.5 115.1 %all-gather.2.cloned.1.call-start = ((), (), s32[]{:S(2)}) async-start(), calls=%async_computation.2 | async-start | bytes 8519680 | tf_op jit(solution)/shard_map/all_gather | solution.py:61
  7.3 235.9 %all-reduce.3.cloned.1.call-start = ((), (), s32[]{:S(2)}) async-start(), calls=%async_computation.3 | async-start | bytes 1048576 | tf_op jit(solution)/shard_map/psum | solution.py:84
  8.1 3.6 copy-start.8
  13.5 108.1 %copy-start.5 = (s32[64,6,128]{2,0,1:T(8,128)}, s32[64,6,128]{2,0,1:T(8,128)S(1)}, u32[]{:S(2)}) copy-start(s32[64,6,128]{2,0,1:T(8,128)S(1)} %reduce-window.19) | copy-start | bytes 589828
  125.6 3.4 copy-start.2
  134.0 3.4 copy-start.2
  142.4 3.4 copy-start.2
  150.8 3.4 copy-start.2
  159.2 3.4 copy-start.2
  167.5 3.4 copy-start.2
  175.9 3.4 copy-start.2
  184.3 3.4 copy-start.2
  190.6 2.6 copy-start.6
  190.6 2.6 copy-start.11
  190.6 2.9 copy-start.9
  191.8 51.3 %copy-start.4 = (bf16[128,2048]{1,0:T(8,128)(2,1)S(1)}, bf16[128,2048]{1,0:T(8,128)(2,1)}, u32[]{:S(2)}) copy-start(bf16[128,2048]{1,0:T(8,128)(2,1)} %param.17) | copy-start | bytes 1572868
  191.8 52.6 %copy-start.10 = (f32[2048]{0:T(1024)S(1)}, f32[2048]{0:T(1024)}, u32[]{:S(2)}) copy-start(f32[2048]{0:T(1024)} %convert_element_type.89) | copy-start | bytes 24580
  247.5 129.1 %copy-start.13 = (bf16[1,2048,352]{1,2,0:T(8,128)(2,1)S(1)}, bf16[1,2048,352]{1,2,0:T(8,128)(2,1)}, u32[]{:S(2)}) copy-start(bf16[1,2048,352]{1,2,0:T(8,128)(2,1)} %param.26) | copy-start | bytes 4325380
  373.9 2.7 copy-start.3
  392.7 9.1 %copy-start.12 = (f32[128,6]{0,1:T(8,128)S(1)}, f32[128,6]{0,1:T(8,128)}, u32[]{:S(2)}) copy-start(f32[128,6]{0,1:T(8,128)} %param.25) | copy-start | bytes 9220
  392.7 9.3 %copy-start.7 = (bf16[2048,352]{0,1:T(8,128)(2,1)S(1)}, bf16[2048,352]{0,1:T(8,128)(2,1)}, u32[]{:S(2)}) copy-start(bf16[2048,352]{0,1:T(8,128)(2,1)} %param.29) | copy-start | bytes 4325380
  392.7 149.6 %all-to-all-start.1 = ((bf16[64,24,2048]{2,1,0:T(8,128)(2,1)}), bf16[64,24,2048]{2,1,0:T(8,128)(2,1)}, u32[]{:S(2)}, u32[]{:S(2)}) async-start(bf16[64,24,2048]{2,1,0:T(8,128)(2,1)} %bitcast.104), calls=%async_computation.1 | async-start | bytes 12582912 | tf_op jit(solution)/shard_map/all_to_all | solution.py:121
  401.4 224.3 %all-reduce.5.cloned.1.call-start = ((), (), s32[]{:S(2)}) async-start(), calls=%async_computation.4 | async-start | bytes 1048576 | tf_op jit(solution)/shard_map/psum | solution.py:127
  567.1 60.8 %copy-start.1 = (bf16[512,2048]{1,0:T(8,128)(2,1)S(1)}, bf16[512,2048]{1,0:T(8,128)(2,1)}, u32[]{:S(2)}) copy-start(bf16[512,2048]{1,0:T(8,128)(2,1)} %param.22) | copy-start | bytes 6291460
Sparse Core Ops, SparseCore 0:
  10.6 110.9 all-gather.1
  193.3 49.7 all-reduce.2
  571.8 53.8 all-reduce.4
where the time goes:
time: 635 us; the launch traced here: 634 us
  waiting for transfers between devices  348 us (55%)
  blocking collectives  126 us (20%)
  matrix products  56.4 us (9%)
  other arithmetic  44.3 us (7%)
  local copies, waits for them, and re-layouts  36.5 us (6%)
  between operations  13.4 us (2%)
  starting transfers between devices  8.99 us (1%)
    all_to_all x1, waiting for transfers between devices, on_device(): lax.all_to_all(finish_partial_out, 'exp', split_axis=0, concat_axis=0, ti...  140 us
    all_to_all x1, blocking collectives, on_device(): lax.all_to_all(buffer, 'exp', split_axis=0, concat_axis=0, tiled=True)  126 us
    all_gather x1, waiting for transfers between devices, on_device(): portion = lax.all_gather(prefix_kv, 'exp', axis=1, tiled=True)  105 us
    psum x1, waiting for transfers between devices, on_device(): lax.psum((shared_part + routed).astype(jnp.bfloat16), 'req')  54 us
    psum x1, waiting for transfers between devices, on_device(): lax.psum(attn_terms.astype(jnp.bfloat16), 'req').astype(jnp.float32)  48.7 us
    reduce_sum x9, other arithmetic, absorb(): new_sum = running_sum * factor + jnp.sum(exp_scores, axis=-1)  25.3 us
    dot_general x9, matrix products, absorb(): jnp.einsum('htd,kd->htk', query_heads, key_rows, preferred_element_type=j...  23.7 us
  transfers between devices with their start and end apart: 4, of which 4 were waited for; matrix products, arithmetic and copies ran while one was open for 2% of the time, Pallas kernels for 0%

commit v1 on v0

--- a/solution.py
+++ b/solution.py
@@ -58,7 +58,11 @@
         )
         return (new_max, new_sum, new_acc)
 
-    portion = lax.all_gather(prefix_kv, "exp", axis=1, tiled=True)
+    derive_leaves = lambda view, lane_axis: jnp.concatenate(
+        lax.all_to_all(jnp.stack(lax.axis_size(lane_axis) * [view], axis=0), lane_axis, 0, 0),
+        axis=1,
+    )
+    portion = derive_leaves(prefix_kv, "exp")
     key_count = portion.shape[1]
     window_len = math.gcd(key_count, 2048)
 

time: 635 us -> 733 us (1.15)
  waiting for transfers between devices: 348 us -> 419 us
  matrix products: 56.4 us -> 81.4 us
  starting transfers between devices: 8.99 us -> 24.5 us
  local copies, waits for them, and re-layouts: 36.5 us -> 27.4 us
    all_to_all x0 -> x1, waiting for transfers between devices: none -> 175 us  [on_device(): lax.all_to_all(jnp.stack(lax.axis_size(lane_axis) * [view], axis=0), lane...]
    all_gather x1 -> x0, waiting for transfers between devices: 105 us -> none  [on_device(): portion = lax.all_gather(prefix_kv, 'exp', axis=1, tiled=True)]
    dot_general x9, matrix products: 8.56 us -> 26.7 us  [absorb(): jnp.einsum('htk,kd->htd', exp_scores.astype(jnp.bfloat16), value_rows, pr...]
    all_to_all x0 -> x1, starting transfers between devices: none -> 15.5 us  [on_device(): lax.all_to_all(jnp.stack(lax.axis_size(lane_axis) * [view], axis=0), lane...]
    dynamic_slice x8 -> x0, local copies, waits for them, and re-layouts: 10.4 us -> none  [inner(): lax.dynamic_slice_in_dim(portion[0], position * window_len, window_len, 0)]
  transfers between devices with their start and end apart: 4 -> 4, of which waited for: 4 -> 4; matrix products, arithmetic and copies ran while one was open for 2% -> 1% of each run, Pallas kernels for 0% -> 0%
where the time goes in v1:
time: 733 us; the launch traced here: 732 us
  waiting for transfers between devices  419 us (57%)
  blocking collectives  126 us (17%)
  matrix products  81.4 us (11%)
  other arithmetic  40 us (5%)
  local copies, waits for them, and re-layouts  27.4 us (4%)
  starting transfers between devices  24.5 us (3%)
  between operations  13.7 us (2%)
    all_to_all x1, waiting for transfers between devices, on_device(): lax.all_to_all(jnp.stack(lax.axis_size(lane_axis) * [view], axis=0), lane...  175 us
    all_to_all x1, waiting for transfers between devices, on_device(): lax.all_to_all(finish_partial_out, 'exp', split_axis=0, concat_axis=0, ti...  139 us
    all_to_all x1, blocking collectives, on_device(): lax.all_to_all(buffer, 'exp', split_axis=0, concat_axis=0, tiled=True)  126 us
    psum x1, waiting for transfers between devices, on_device(): lax.psum((shared_part + routed).astype(jnp.bfloat16), 'req')  56.8 us
    psum x1, waiting for transfers between devices, on_device(): lax.psum(attn_terms.astype(jnp.bfloat16), 'req').astype(jnp.float32)  47.9 us
    dot_general x9, matrix products, absorb(): jnp.einsum('htd,kd->htk', query_heads, key_rows, preferred_element_type=j...  30.7 us
    dot_general x9, matrix products, absorb(): jnp.einsum('htk,kd->htd', exp_scores.astype(jnp.bfloat16), value_rows, pr...  26.7 us
    reduce_sum x9, other arithmetic, absorb(): new_sum = running_sum * factor + jnp.sum(exp_scores, axis=-1)  24.1 us
  transfers between devices with their start and end apart: 4, of which 4 were waited for; matrix products, arithmetic and copies ran while one was open for 1% of the time, Pallas kernels for 0%

profile of v1, /device:TPU:1, one launch (start us, length us, event | category | flops | bytes accessed | tf_op | source)
XLA Modules:
  0.0 732.2 jit_solution(4102215810174382764)
XLA Ops:
  6.5 5.3 stack.2
  11.8 15.5 %all-to-all-start = ((bf16[64,1,256,256]{3,2,1,0:T(8,128)(2,1)}), bf16[64,1,256,256]{3,2,1,0:T(8,128)(2,1)}, u32[]{:S(2)}, u32[]{:S(2)}) async-start(bf16[64,1,256,256]{3,2,1,0:T(8,128)(2,1)} %stack.2), calls=%async_computation | async-start | bytes 16777216 | tf_op jit(solution)/shard_map/all_to_all | solution.py:62
  31.5 175.4 %all-to-all-done = bf16[64,1,256,256]{3,2,1,0:T(8,128)(2,1)} async-done(((bf16[64,1,256,256]{3,2,1,0:T(8,128)(2,1)}), bf16[64,1,256,256]{3,2,1,0:T(8,128)(2,1)}, u32[]{:S(2)}, u32[]{:S(2)}) %all-to-all-start) | async-done | bytes 8388640 | tf_op jit(solution)/shard_map/all_to_all | solution.py:62
  206.9 78.9 %while.18 = (s32[]{:T(128)}, f32[4,128]{1,0:T(4,128)S(1)}, f32[4,128]{1,0:T(4,128)S(1)}, f32[4,128,128]{2,1,0:T(8,128)S(1)}, bf16[64,1,256,256]{3,2,0,1:T(8,128)...) while((s32[]{:T(128)}, f32[4,128]{1,0:T(4,128)S(1)}, ...), condition=%wide.region_3.0_spmd.clone, body=%wide.region_0.0_spmd.clone.sunk | while | flops 545458688 | bytes 14319807 | solution.py:73
  206.9 3.7 bitcast_reduce_fusion.2
  210.6 2.9 fusion.76
  213.5 3.2 fusion.78
  216.7 3.7 bitcast_reduce_fusion.2
  223.3 3.2 fusion.78
  226.6 3.7 bitcast_reduce_fusion.2
  233.2 3.2 fusion.78
  236.4 3.7 bitcast_reduce_fusion.2
  243.1 3.2 fusion.78
  246.3 3.7 bitcast_reduce_fusion.2
  252.9 3.2 fusion.78
  256.2 3.7 bitcast_reduce_fusion.2
  262.8 3.2 fusion.78
  266.0 3.7 bitcast_reduce_fusion.2
  272.6 3.2 fusion.78
  275.9 3.7 bitcast_reduce_fusion.2
  282.5 3.2 fusion.78
  291.3 47.9 %all-reduce.3.cloned.1.call-done = bf16[128,2048]{1,0:T(8,128)(2,1)} async-done(((bf16[128,2048]{1,0:T(8,128)(2,1)}), bf16[128,2048]{1,0:T(8,128)(2,1)}) %all-reduce.3.cloned.1.call-update) | async-done | bytes 524304 | tf_op jit(solution)/shard_map/psum | solution.py:88
  343.6 126.2 %all_to_all.15 = bf16[64,24,2048]{2,1,0:T(8,128)(2,1)S(1)} all-to-all(bf16[64,24,2048]{2,1,0:T(8,128)(2,1)S(1)} %bitcast.104), channel_id=1, replica_groups=mesh['req'=4,'exp'=64] {'exp'}, dimensions={0} | all-to-all | bytes 12582912 | tf_op jit(solution)/shard_map/all_to_all | solution.py:115
  472.5 3.8 fusion.19
  476.4 12.3 %convolution_convert_fusion = bf16[1536,2048]{1,0:T(8,128)(2,1)} fusion(bf16[1,352,2048]{2,1,0:T(8,128)(2,1)} %param.28, bf16[1536,2048]{1,0:T(8,128)(2,1)} %bitcast.107, f32[1536,352]{0,1:T(8,128)} %fusion.19, bf16[1,2048,352]{1,2,0:T(8,128)(2,1)} %param.27), kind=kOutput, calls=%fused_computation.21 | convolution fusion | flops 4435574784 | bytes 17629184 | tf_op jit(solution)/shard_map/dot_general | solution.py:121
  488.6 8.6 %all-to-all-start.2 = ((bf16[64,24,2048]{2,1,0:T(8,128)(2,1)}), bf16[64,24,2048]{2,1,0:T(8,128)(2,1)}, u32[]{:S(2)}, u32[]{:S(2)}) async-start(bf16[64,24,2048]{2,1,0:T(8,128)(2,1)} %bitcast.105), calls=%async_computation.2 | async-start | bytes 12582912 | tf_op jit(solution)/shard_map/all_to_all | solution.py:125
  498.4 138.5 %all-to-all-done.2 = bf16[64,24,2048]{2,1,0:T(8,128)(2,1)} async-done(((bf16[64,24,2048]{2,1,0:T(8,128)(2,1)}), bf16[64,24,2048]{2,1,0:T(8,128)(2,1)}, u32[]{:S(2)}, u32[]{:S(2)}) %all-to-all-start.2) | async-done | bytes 6291488 | tf_op jit(solution)/shard_map/all_to_all | solution.py:125
  636.9 10.7 %gather_fusion = bf16[768,2048]{1,0:T(8,128)(2,1)} fusion(bf16[1536,2048]{1,0:T(8,128)(2,1)} %bitcast.20, s32[1024]{0:T(1024)S(1)} %pad_clamp_fusion), kind=kCustom, calls=%fused_computation | custom fusion | bytes 6294528 | tf_op jit(solution)/shard_map/gather | solution.py:128
  647.6 6.6 reshape.163
  654.2 7.8 %multiply_reduce_fusion = f32[128,2048]{1,0:T(8,128)} fusion(f32[128,6,2048]{2,1,0:T(8,128)} %reshape.163, f32[128,6]{1,0:T(8,128)S(1)} %copy.60), kind=kLoop, calls=%fused_computation.20 | loop fusion | flops 2883584 | bytes 7343104 | tf_op jit(solution)/shard_map/reduce_sum | solution.py:130
  661.9 4.4 fusion.16
  666.3 56.8 %all-reduce.5.cloned.1.call-done = bf16[128,2048]{1,0:T(8,128)(2,1)} async-done(((bf16[128,2048]{1,0:T(8,128)(2,1)}), bf16[128,2048]{1,0:T(8,128)(2,1)}) %all-reduce.5.cloned.1.call-update) | async-done | bytes 524304 | tf_op jit(solution)/shard_map/psum | solution.py:131
  (97 shorter events, 40.3 us)
Async XLA Ops:
  6.5 282.3 %copy-start = (bf16[512,2048]{1,0:T(8,128)(2,1)S(1)}, bf16[512,2048]{1,0:T(8,128)(2,1)}, u32[]{:S(2)}) copy-start(bf16[512,2048]{1,0:T(8,128)(2,1)} %param.22) | copy-start | bytes 6291460
  11.8 15.6 %copy-start.7 = (s32[128,6]{0,1:T(8,128)S(1)}, s32[128,6]{0,1:T(8,128)}, u32[]{:S(2)}) copy-start(s32[128,6]{0,1:T(8,128)} %param.24) | copy-start | bytes 9220
  11.8 16.0 %copy-start.5 = (bf16[128,512]{1,0:T(8,128)(2,1)S(1)}, bf16[128,512]{1,0:T(8,128)(2,1)}, u32[]{:S(2)}) copy-start(bf16[128,512]{1,0:T(8,128)(2,1)} %param.18) | copy-start | bytes 393220
  11.8 16.3 %copy-start.11 = (s32[1,4]{1,0:T(1,128)S(1)}, s32[1,4]{1,0:T(1,128)}, u32[]{:S(2)}) copy-start(s32[1,4]{1,0:T(1,128)} %param.21) | copy-start | bytes 52
  11.8 16.5 %copy-start.8 = (bf16[2048]{0:T(1024)(128)(2,1)S(1)}, bf16[2048]{0:T(1024)(128)(2,1)}, u32[]{:S(2)}) copy-start(bf16[2048]{0:T(1024)(128)(2,1)} %param.23) | copy-start | bytes 12292
  11.8 18.8 %copy-start.6 = (bf16[128,1,256]{2,0,1:T(8,128)(2,1)S(1)}, bf16[128,1,256]{2,0,1:T(8,128)(2,1)}, u32[]{:S(2)}) copy-start(bf16[128,1,256]{2,0,1:T(8,128)(2,1)} %param.20) | copy-start | bytes 196612
  11.8 195.0 %all-to-all-start = ((bf16[64,1,256,256]{3,2,1,0:T(8,128)(2,1)}), bf16[64,1,256,256]{3,2,1,0:T(8,128)(2,1)}, u32[]{:S(2)}, u32[]{:S(2)}) async-start(bf16[64,1,256,256]{3,2,1,0:T(8,128)(2,1)} %stack.2), calls=%async_computation | async-start | bytes 16777216 | tf_op jit(solution)/shard_map/all_to_all | solution.py:62
  27.4 311.9 %all-reduce.3.cloned.1.call-start = ((), (), s32[]{:S(2)}) async-start(), calls=%async_computation.3 | async-start | bytes 1048576 | tf_op jit(solution)/shard_map/psum | solution.py:88
  285.7 53.6 %copy-start.3 = (bf16[128,2048]{1,0:T(8,128)(2,1)S(1)}, bf16[128,2048]{1,0:T(8,128)(2,1)}, u32[]{:S(2)}) copy-start(bf16[128,2048]{1,0:T(8,128)(2,1)} %param.17) | copy-start | bytes 1572868
  343.6 128.9 %copy-start.10 = (bf16[1,2048,352]{1,2,0:T(8,128)(2,1)S(1)}, bf16[1,2048,352]{1,2,0:T(8,128)(2,1)}, u32[]{:S(2)}) copy-start(bf16[1,2048,352]{1,2,0:T(8,128)(2,1)} %param.26) | copy-start | bytes 4325380
  469.9 2.7 copy-start.2
  488.6 9.1 %copy-start.9 = (f32[128,6]{0,1:T(8,128)S(1)}, f32[128,6]{0,1:T(8,128)}, u32[]{:S(2)}) copy-start(f32[128,6]{0,1:T(8,128)} %param.25) | copy-start | bytes 9220
  488.6 9.2 %copy-start.4 = (bf16[2048,352]{0,1:T(8,128)(2,1)S(1)}, bf16[2048,352]{0,1:T(8,128)(2,1)}, u32[]{:S(2)}) copy-start(bf16[2048,352]{0,1:T(8,128)(2,1)} %param.29) | copy-start | bytes 4325380
  488.6 148.3 %all-to-all-start.2 = ((bf16[64,24,2048]{2,1,0:T(8,128)(2,1)}), bf16[64,24,2048]{2,1,0:T(8,128)(2,1)}, u32[]{:S(2)}, u32[]{:S(2)}) async-start(bf16[64,24,2048]{2,1,0:T(8,128)(2,1)} %bitcast.105), calls=%async_computation.2 | async-start | bytes 12582912 | tf_op jit(solution)/shard_map/all_to_all | solution.py:125
  497.3 225.8 %all-reduce.5.cloned.1.call-start = ((), (), s32[]{:S(2)}) async-start(), calls=%async_computation.4 | async-start | bytes 1048576 | tf_op jit(solution)/shard_map/psum | solution.py:131
  654.2 71.2 %copy-start.1 = (bf16[512,2048]{1,0:T(8,128)(2,1)S(1)}, bf16[512,2048]{1,0:T(8,128)(2,1)}, u32[]{:S(2)}) copy-start(bf16[512,2048]{1,0:T(8,128)(2,1)} %param.22) | copy-start | bytes 6291460
Sparse Core Ops, SparseCore 0:
  290.3 48.9 all-reduce.2
  666.4 56.6 all-reduce.4
